TPU v7x, 32 devices: a whole 2x2x4 slice. The times are simulated.
32 devices in a mesh: seq: 8 (over z, y), head: 4 (over x, core).
Axes of the slice: x: 2, y: 2, z: 4, core: 2. Of those that a mesh axis runs over, the one named last changes fastest.
Arguments:
- queries: bfloat16 [1024, 3584], P('seq', 'head'), may hold values from -256 to 256
- key_codes: bfloat16 [1024, 512], P('seq', 'head'), may hold values from -4 to 4
- value_codes: bfloat16 [1024, 512], P('seq', 'head'), may hold values from -4 to 4
- kv_scales: float32 [2, 8, 4], P(None, 'seq', 'head'), may hold values from 0.5 to 2
- out_weight: bfloat16 [3584, 3584], P('head'), may hold values from -0.09375 to 0.09375
- turn_ids: int32 [1024], replicated, may hold values from 0 to 7, never falling along the last dimension, each value on 1 to 256 neighbouring positions
- block_mask: int32 [8, 8], P('seq'), may hold values 0 or 1
- doc_lengths: int32 [4], replicated, may hold values from 1 to 512, 1024 in all
Outputs:
- projected: bfloat16 [1024, 3584], P('seq', 'head')
All inputs are finite; a program needn't handle non-finite values. No bound on the sum of `block_mask` on one device may be relied on, other than what follows from the above.
Results may differ from a plain program's by a relative error of at most 0.012.
Values may be sent and summed in bfloat16 or wider, within the bound.
No kernel may reach another device: no remote copies, remote signals or barrier semaphores. Data moves between devices by JAX's collectives and lax.ppermute only.
A program may use at most 128 MiB of HBM per device.

v0:
```python
import math
import jax
import jax.numpy as jnp
from jax import lax
from jax.sharding import PartitionSpec as P

HEAD_DIM = 128
BLOCK = 128
masked_score = -1e30


def document_of(places, doc_lengths):
    ends = jnp.cumsum(doc_lengths)
    return jnp.sum((places[:, None] >= ends[None, :]).astype(jnp.int32), axis=1)


def dequantize(codes, scales):
    blocks = scales.shape[0]
    shaped = codes.astype(jnp.float32).reshape(blocks, -1, codes.shape[1])
    return (shaped * scales[:, None, None]).reshape(codes.shape).astype(jnp.bfloat16)


def on_device(
    queries, key_codes, value_codes, kv_scales, out_weight, turn_ids, block_mask, doc_lengths
):
    row_count = queries.shape[0]
    groups = queries.shape[1] // HEAD_DIM
    mine = lax.axis_index("seq")
    scaling = 1.0 / math.sqrt(HEAD_DIM)
    keys = dequantize(key_codes, kv_scales[0, :, 0])
    values = dequantize(value_codes, kv_scales[1, :, 0])
    key_value = jnp.stack([keys, values])
    query_heads = queries.reshape(row_count, groups, HEAD_DIM)
    offsets = jnp.arange(row_count, dtype=jnp.int32)
    query_places = mine * row_count + offsets
    query_turns = lax.dynamic_slice_in_dim(turn_ids, mine * row_count, row_count)
    query_docs = document_of(query_places, doc_lengths)
    mask_rows = block_mask[offsets // BLOCK]
    pair = lax.all_gather(key_value, "seq", axis=1, tiled=True)
    width = pair.shape[1]
    key_places = jnp.arange(width, dtype=jnp.int32)
    key_docs = document_of(key_places, doc_lengths)
    kept = jnp.take(mask_rows, key_places // BLOCK, axis=1) > 0
    same_block = (query_places // BLOCK)[:, None] == (key_places // BLOCK)[None, :]
    allowed = (
        (key_places[None, :] <= query_places[:, None])
        & (query_docs[:, None] == key_docs[None, :])
        & ((query_turns[:, None] == turn_ids[None, :]) | kept | same_block)
    )
    best = jnp.full((groups, row_count), masked_score, jnp.float32)
    scores = (
        jnp.einsum("qgd,kd->gqk", query_heads, pair[0], preferred_element_type=jnp.float32)
        * scaling
    )
    scores = jnp.where(allowed[None], scores, masked_score)
    newest = jnp.maximum(best, jnp.max(scores, axis=2))
    weights = jnp.where(allowed[None], jnp.exp(scores - newest[:, :, None]), 0.0)
    totals = jnp.sum(weights, axis=2)
    summed = jnp.einsum(
        "gqk,kd->gqd", weights.astype(jnp.bfloat16), pair[1], preferred_element_type=jnp.float32
    )
    state = (newest, totals, summed)
    best, totals, summed = state
    attended = (summed / totals[:, :, None]).astype(jnp.bfloat16)
    weight_heads = out_weight.reshape(groups, HEAD_DIM, out_weight.shape[1])
    partial_value = jnp.einsum(
        "gqd,gde->qe", attended, weight_heads, preferred_element_type=jnp.float32
    )
    return lax.psum_scatter(
        partial_value.astype(jnp.bfloat16), "head", scatter_dimension=1, tiled=True
    )


def solution(mesh):
    placed = (
        P("seq", "head"),
        P("seq", "head"),
        P("seq", "head"),
        P(None, "seq", "head"),
        P("head", None),
        P(),
        P("seq", None),
        P(),
    )
    return jax.shard_map(
        on_device, mesh=mesh, in_specs=placed, out_specs=P("seq", "head"), check_vma=False
    )
```

profile of v0, /device:TPU:0, one launch (start us, length us, event | category | flops | bytes accessed | tf_op | source)
XLA Modules:
  0.0 95.0 jit_solution(5045930761843892157)
XLA Ops:
  6.5 0.0 copy-start
  6.5 0.0 copy-start.2
  6.5 0.0 reduce-scatter.4.cloned.1.call-start
  6.6 0.8 reduce-window.8
  7.4 0.1 convert_reduce_fusion
  7.5 0.1 convert_reduce_fusion.1
  7.6 1.4 %fusion.33 = (f32[1,1,1]{0,2,1:T(1,128)}, f32[1,1,1]{0,2,1:T(1,128)}) fusion(f32[2,1,1]{0,2,1:T(1,128)} %param.11), kind=kLoop, calls=%fused_computation.55 | loop fusion | bytes 16 | tf_op jit(solution)/shard_map/slice | solution.py:30
  9.0 1.1 %copy.15 = bf16[128,896]{0,1:T(8,128)(2,1)S(1)} copy(bf16[128,896]{1,0:T(8,128)(2,1)} %param.8) | data formatting | bytes 458752 | tf_op args[0]
  10.1 2.1 %fusion.22 = (bf16[1,128,128]{2,1,0:T(8,128)(2,1)S(1)}, bf16[1,128,128]{2,1,0:T(8,128)(2,1)S(1)}) fusion(bf16[128,128]{1,0:T(8,128)(2,1)} %param.9, f32[]{:T(128)} %bitcast.5, f32[]{:T(128)} %bitcast.7, bf16[128,128]{1,0:T(8,128)(2,1)} %param.10), kind=kLoop, calls=%fused_computation.26 | loop fusion | flops 98304 | bytes 131080 | tf_op jit(solution)/shard_map/convert_element_type | solution.py:20
  12.2 33.0 %all_gather.3 = bf16[2,1024,128]{2,1,0:T(8,128)(2,1)S(1)} all-gather(bf16[2,128,128]{2,1,0:T(8,128)(2,1)S(1)} %pad_maximum_fusion), channel_id=1, replica_groups=mesh['seq'=8,'head'=4] {'seq'}, dimensions={1}, use_global_device_ids=true | all-gather | bytes 589824 | tf_op jit(solution)/shard_map/all_gather | solution.py:39
  45.3 0.8 dynamic_slice.3
  46.0 0.0 copy-done
  46.0 0.1 broadcast.312
  46.1 2.8 %gather_fusion = s32[1024,128]{1,0:T(8,128)S(1)} fusion(s32[128,8]{0,1:T(8,128)S(1)} %broadcast.312, s32[1024]{0:T(1024)S(1)} %broadcast_clamp_fusion), kind=kCustom, calls=%fused_computation | custom fusion | bytes 1052672 | tf_op jit(solution)/shard_map/jit(_take)/gather | solution.py:43
  48.9 0.0 copy-done.2
  48.9 1.0 %fusion.16 = pred[128,1024]{0,1:T(8,128)(4,1)S(1)} fusion(s32[1024,128]{1,0:T(8,128)S(1)} %gather_fusion, s32[128]{0:T(128)S(1)} %get-tuple-element.9, s32[128]{0:T(128)S(1)} %dynamic_slice.3, s32[128]{0:T(128)S(1)} %convert_reduce_fusion.1, s32[128]{0:T(128)S(1)} %get-tuple-element.10, s32[1024]{0:T(1024)S(1)} %add_select_fusion, s32[1024]{0:T(1024)S(1)} %copy-done.2, ...), kind=kLoop, calls=%fused_computation.15 | loop fusion | flops 1310720 | bytes 670720 | tf_op jit(solution)/shard_map/and | solution.py:46
  50.0 0.7 fusion.1
  50.6 0.0 copy-start.1
  50.7 1.8 %copy-done.1 = f32[1024,128,7]{1,0,2:T(8,128)} copy-done((f32[1024,128,7]{1,0,2:T(8,128)}, f32[1024,128,7]{1,0,2:T(8,128)S(1)}, u32[]{:S(2)}) %copy-start.1) | copy-done | bytes 3670040
  52.4 0.9 fusion.2
  53.3 6.5 %fusion = bf16[128,3584]{1,0:T(8,128)(2,1)S(1)} fusion(bf16[7,128,3584]{2,1,0:T(8,128)(2,1)} %bitcast.63, f32[1024,128,7]{1,0,2:T(8,128)} %copy-done.1, f32[7,128]{1,0:T(8,128)S(1)} %broadcast_maximum_fusion, pred[128,1024]{0,1:T(8,128)(4,1)S(1)} %fusion.16, bf16[2,1024,128]{2,1,0:T(8,128)(2,1)S(1)} %all_gather.3, f32[7,128]{1,0:T(8,128)S(1)} %fusion.2), kind=kOutput, calls=%fused_computation.2 | convolution fusion | flops 1062240256 | bytes 11411456 | tf_op jit(solution)/shard_map/gqd,gde->qe/dot_general | solution.py:66
  59.8 1.3 %copy.20 = bf16[128,3584]{0,1:T(8,128)(2,1)} copy(bf16[128,3584]{1,0:T(8,128)(2,1)S(1)} %fusion) | data formatting | bytes 1835008
  61.1 0.0 reduce-scatter.4.cloned.1.call-update
  61.1 25.2 %reduce-scatter.4.cloned.1.call-done = bf16[896,128]{1,0:T(8,128)(2,1)} async-done(((bf16[3584,128]{1,0:T(8,128)(2,1)}), bf16[896,128]{1,0:T(8,128)(2,1)}) %reduce-scatter.4.cloned.1.call-update) | async-done | bytes 229392
  86.4 1.8 %copy.21 = bf16[128,896]{1,0:T(8,128)(2,1)} copy(bf16[128,896]{0,1:T(8,128)(2,1)} %bitcast.59) | data formatting | bytes 458752
  (7 shorter events, 0.0 us)
Async XLA Ops:
  6.5 39.5 %copy-start = (s32[1,8]{1,0:T(1,128)S(1)}, s32[1,8]{1,0:T(1,128)}, u32[]{:S(2)}) copy-start(s32[1,8]{1,0:T(1,128)} %param.14) | copy-start | bytes 100
  6.5 42.4 %copy-start.2 = (s32[1024]{0:T(1024)S(1)}, s32[1024]{0:T(1024)}, u32[]{:S(2)}) copy-start(s32[1024]{0:T(1024)} %param.13) | copy-start | bytes 12292
  6.5 79.8 %reduce-scatter.4.cloned.1.call-start = ((), (), s32[]{:S(2)}) async-start(), calls=%async_computation.1 | async-start | bytes 1146880
  50.6 1.8 %copy-start.1 = (f32[1024,128,7]{1,0,2:T(8,128)}, f32[1024,128,7]{1,0,2:T(8,128)S(1)}, u32[]{:S(2)}) copy-start(f32[1024,128,7]{1,0,2:T(8,128)S(1)} %get-tuple-element.8) | copy-start | bytes 11010052
Sparse Core Ops, SparseCore 0:
  61.2 25.0 reduce-scatter.3
where the time goes:
time: 95.3 us; the launch traced here: 95 us
  blocking collectives  33 us (35%)
  waiting for transfers between devices  25.3 us (27%)
  between operations  13.5 us (14%)
  local copies, waits for them, and re-layouts  11 us (12%)
  matrix products  7.15 us (8%)
  other arithmetic  5.07 us (5%)
    all_gather x1, blocking collectives, on_device(): pair = lax.all_gather(key_value, 'seq', axis=1, tiled=True)  33 us
    unnamed x2, waiting for transfers between devices  25.3 us
    dot_general x1, matrix products, on_device(): jnp.einsum('gqd,gde->qe', attended, weight_heads, preferred_element_type=...  6.46 us
    unnamed x9, local copies, waits for them, and re-layouts  5.94 us
    gather x1, local copies, waits for them, and re-layouts, on_device(): kept = jnp.take(mask_rows, key_places // BLOCK, axis=1) > 0  2.81 us
    convert_element_type x1, other arithmetic, dequantize(): (shaped * scales[:, None, None]).reshape(codes.shape).astype(jnp.bfloat16)  2.13 us
  transfers between devices with their start and end apart: 1, of which 1 were waited for; matrix products, arithmetic and copies ran while one was open for 0% of the time, Pallas kernels for 0%

commit v1 on v0

--- a/solution.py
+++ b/solution.py
@@ -7,6 +7,23 @@
 HEAD_DIM = 128
 BLOCK = 128
 masked_score = -1e30
+
+
+def in_order(blocks, dim):
+    shape = list(blocks.shape[1:])
+    shape[dim] *= blocks.shape[0]
+    return jnp.moveaxis(blocks, 0, dim).reshape(shape)
+
+
+def grow_blocks(shard, axis):
+    size, index = (lax.axis_size(axis), lax.axis_index(axis))
+    blocks, bit = (shard[None], 1)
+    while bit < size:
+        other = lax.ppermute(blocks, axis, [(i, i ^ bit) for i in range(size)])
+        low = index & bit == 0
+        blocks = jnp.concatenate([jnp.where(low, blocks, other), jnp.where(low, other, blocks)])
+        bit *= 2
+    return blocks
 
 
 def document_of(places, doc_lengths):
@@ -36,7 +53,7 @@
     query_turns = lax.dynamic_slice_in_dim(turn_ids, mine * row_count, row_count)
     query_docs = document_of(query_places, doc_lengths)
     mask_rows = block_mask[offsets // BLOCK]
-    pair = lax.all_gather(key_value, "seq", axis=1, tiled=True)
+    pair = in_order(grow_blocks(key_value, "seq"), 1)
     width = pair.shape[1]
     key_places = jnp.arange(width, dtype=jnp.int32)
     key_docs = document_of(key_places, doc_lengths)

time: 95.3 us -> 78.9 us (0.83)
  blocking collectives: 33 us -> 0 us
  starting transfers between devices: 0.01 us -> 8.3 us
  waiting for transfers between devices: 25.3 us -> 33.3 us
    all_gather x1 -> x0, blocking collectives: 33 us -> none  [on_device(): pair = lax.all_gather(key_value, 'seq', axis=1, tiled=True)]
    ppermute x0 -> x3, starting transfers between devices: none -> 8.3 us  [grow_blocks(): other = lax.ppermute(blocks, axis, [(i, i ^ bit) for i in range(size)])]
    ppermute x0 -> x3, waiting for transfers between devices: none -> 7.98 us  [grow_blocks(): other = lax.ppermute(blocks, axis, [(i, i ^ bit) for i in range(size)])]
  transfers between devices with their start and end apart: 1 -> 4, of which waited for: 1 -> 4; matrix products, arithmetic and copies ran while one was open for 0% -> 9% of each run, Pallas kernels for 0% -> 0%
where the time goes in v1:
time: 78.9 us; the launch traced here: 78.6 us
  waiting for transfers between devices  33.3 us (42%)
  between operations  13.5 us (17%)
  local copies, waits for them, and re-layouts  11 us (14%)
  starting transfers between devices  8.3 us (11%)
  matrix products  7.16 us (9%)
  other arithmetic  5.24 us (7%)
    unnamed x2, waiting for transfers between devices  25.4 us
    ppermute x3, starting transfers between devices, grow_blocks(): other = lax.ppermute(blocks, axis, [(i, i ^ bit) for i in range(size)])  8.3 us
    ppermute x3, waiting for transfers between devices, grow_blocks(): other = lax.ppermute(blocks, axis, [(i, i ^ bit) for i in range(size)])  7.98 us
    dot_general x1, matrix products, on_device(): jnp.einsum('gqd,gde->qe', attended, weight_heads, preferred_element_type=...  6.47 us
    unnamed x9, local copies, waits for them, and re-layouts  5.94 us
    gather x1, local copies, waits for them, and re-layouts, on_device(): kept = jnp.take(mask_rows, key_places // BLOCK, axis=1) > 0  2.81 us
    convert_element_type x1, other arithmetic, dequantize(): (shaped * scales[:, None, None]).reshape(codes.shape).astype(jnp.bfloat16)  2.12 us
  transfers between devices with their start and end apart: 4, of which 4 were waited for; matrix products, arithmetic and copies ran while one was open for 9% of the time, Pallas kernels for 0%

profile of v1, /device:TPU:0, one launch (start us, length us, event | category | flops | bytes accessed | tf_op | source)
XLA Modules:
  0.0 78.6 jit_solution(617980751805996241)
XLA Ops:
  6.5 0.0 copy-start
  6.5 0.0 copy-start.2
  6.5 0.0 reduce-scatter.4.cloned.1.call-start
  6.5 1.4 %fusion.33 = (f32[1,1,1]{0,2,1:T(1,128)}, f32[1,1,1]{0,2,1:T(1,128)}) fusion(f32[2,1,1]{0,2,1:T(1,128)} %param.11), kind=kLoop, calls=%fused_computation.62 | loop fusion | bytes 16 | tf_op jit(solution)/shard_map/slice | solution.py:47
  7.9 2.1 %fusion.21 = (bf16[1,128,128]{2,1,0:T(8,128)(2,1)S(1)}, bf16[1,128,128]{2,1,0:T(8,128)(2,1)S(1)}) fusion(bf16[128,128]{1,0:T(8,128)(2,1)} %param.9, f32[]{:T(128)} %bitcast.5, f32[]{:T(128)} %bitcast.7, bf16[128,128]{1,0:T(8,128)(2,1)} %param.10), kind=kLoop, calls=%fused_computation.32 | loop fusion | flops 98304 | bytes 131080 | tf_op jit(solution)/shard_map/convert_element_type | solution.py:37
  10.1 3.1 %collective-permute-start = (bf16[1,2,128,128]{3,2,1,0:T(8,128)(2,1)S(1)}, bf16[1,2,128,128]{3,2,1,0:T(8,128)(2,1)S(1)}, u32[]{:S(2)}, u32[]{:S(2)}) collective-permute-start(bf16[1,2,128,128]{3,2,1,0:T(8,128)(2,1)S(1)} %maximum_bitcast_fusion.1), channel_id=1, source_target_pairs={{0,4},{4,0},{8,12},{12,8},{16,20},{20,16},{24,28},{28,24},{1,5},{5... | collective-permute-start | bytes 196616 | tf_op jit(solution)/shard_map/ppermute | solution.py:22
  13.1 0.8 %reduce-window.8 = s32[4,1]{0,1:T(1,128)S(1)} reduce-window(s32[4,1]{0,1:T(1,128)} %bitcast.71, s32[]{:T(128)} %constant.73.clone.1), window={size=4x1 pad=3_0x0_0}, to_apply=%region_0.0 | reduce-window | flops 12 | bytes 36 | tf_op jit(solution)/shard_map/reduce-window.3
  14.0 0.1 convert_reduce_fusion
  14.1 1.3 %collective-permute-done = bf16[1,2,128,128]{3,2,1,0:T(8,128)(2,1)S(1)} collective-permute-done((bf16[1,2,128,128]{3,2,1,0:T(8,128)(2,1)S(1)}, bf16[1,2,128,128]{3,2,1,0:T(8,128)(2,1)S(1)}, u32[]{:S(2)}, u32[]{:S(2)}) %collective-permute-start) | collective-permute-done | bytes 65568 | tf_op jit(solution)/shard_map/ppermute | solution.py:22
  15.4 2.1 %collective-permute-start.1 = (bf16[2,2,128,128]{3,2,1,0:T(8,128)(2,1)S(1)}, bf16[2,2,128,128]{3,2,1,0:T(8,128)(2,1)S(1)}, u32[]{:S(2)}, u32[]{:S(2)}) collective-permute-start(bf16[2,2,128,128]{3,2,1,0:T(8,128)(2,1)S(1)} %pad_maximum_fusion.1), channel_id=1, source_target_pairs={{0,8},{4,12},{8,0},{12,4},{16,24},{20,28},{24,16},{28,20},{1,9},{5... | collective-permute-start | bytes 393224 | tf_op jit(solution)/shard_map/ppermute | solution.py:22
  17.6 0.1 convert_reduce_fusion.1
  17.7 2.8 %collective-permute-done.1 = bf16[2,2,128,128]{3,2,1,0:T(8,128)(2,1)S(1)} collective-permute-done((bf16[2,2,128,128]{3,2,1,0:T(8,128)(2,1)S(1)}, bf16[2,2,128,128]{3,2,1,0:T(8,128)(2,1)S(1)}, u32[]{:S(2)}, u32[]{:S(2)}) %collective-permute-start.1) | collective-permute-done | bytes 131104 | tf_op jit(solution)/shard_map/ppermute | solution.py:22
  20.6 3.1 %collective-permute-start.2 = (bf16[4,2,128,128]{3,2,1,0:T(8,128)(2,1)S(1)}, bf16[4,2,128,128]{3,2,1,0:T(8,128)(2,1)S(1)}, u32[]{:S(2)}, u32[]{:S(2)}) collective-permute-start(bf16[4,2,128,128]{3,2,1,0:T(8,128)(2,1)S(1)} %pad_maximum_fusion), channel_id=1, source_target_pairs={{0,16},{4,20},{8,24},{12,28},{16,0},{20,4},{24,8},{28,12},{1,17},{... | collective-permute-start | bytes 786440 | tf_op jit(solution)/shard_map/ppermute | solution.py:22
  23.7 1.1 %copy.15 = bf16[128,896]{0,1:T(8,128)(2,1)S(1)} copy(bf16[128,896]{1,0:T(8,128)(2,1)} %param.8) | data formatting | bytes 458752 | tf_op args[0]
  24.8 0.8 dynamic_slice.3
  25.6 0.0 copy-done
  25.6 0.1 broadcast.312
  25.6 2.8 %gather_fusion = s32[1024,128]{1,0:T(8,128)S(1)} fusion(s32[128,8]{0,1:T(8,128)S(1)} %broadcast.312, s32[1024]{0:T(1024)S(1)} %broadcast_clamp_fusion), kind=kCustom, calls=%fused_computation | custom fusion | bytes 1052672 | tf_op jit(solution)/shard_map/jit(_take)/gather | solution.py:60
  28.4 0.0 copy-done.2
  28.4 1.0 %fusion.16 = pred[128,1024]{0,1:T(8,128)(4,1)S(1)} fusion(s32[1024,128]{1,0:T(8,128)S(1)} %gather_fusion, s32[128]{0:T(128)S(1)} %get-tuple-element.19, s32[128]{0:T(128)S(1)} %dynamic_slice.3, s32[128]{0:T(128)S(1)} %convert_reduce_fusion.1, s32[128]{0:T(128)S(1)} %get-tuple-element.20, s32[1024]{0:T(1024)S(1)} %add_select_fusion, s32[1024]{0:T(1024)S(1)} %copy-done.2, ...), kind=kLoop, calls=%fused_computation.16 | loop fusion | flops 1310720 | bytes 670720 | tf_op jit(solution)/shard_map/and | solution.py:63
  29.5 3.8 %collective-permute-done.2 = bf16[4,2,128,128]{3,2,1,0:T(8,128)(2,1)S(1)} collective-permute-done((bf16[4,2,128,128]{3,2,1,0:T(8,128)(2,1)S(1)}, bf16[4,2,128,128]{3,2,1,0:T(8,128)(2,1)S(1)}, u32[]{:S(2)}, u32[]{:S(2)}) %collective-permute-start.2) | collective-permute-done | bytes 262176 | tf_op jit(solution)/shard_map/ppermute | solution.py:22
  33.4 0.7 fusion.1
  34.1 0.0 copy-start.1
  34.2 1.8 %copy-done.1 = f32[1024,128,7]{1,0,2:T(8,128)} copy-done((f32[1024,128,7]{1,0,2:T(8,128)}, f32[1024,128,7]{1,0,2:T(8,128)S(1)}, u32[]{:S(2)}) %copy-start.1) | copy-done | bytes 3670040
  35.9 0.9 %fusion.2 = f32[7,128]{1,0:T(8,128)S(1)} fusion(f32[1024,128,7]{1,0,2:T(8,128)S(1)} %get-tuple-element.16, f32[7,128]{1,0:T(8,128)S(1)} %broadcast_maximum_fusion, pred[128,1024]{0,1:T(8,128)(4,1)S(1)} %fusion.16), kind=kLoop, calls=%fused_computation.6 | loop fusion | flops 4586624 | bytes 3808256 | tf_op jit(solution)/shard_map/reduce_sum | solution.py:75
  36.8 6.5 %fusion = bf16[128,3584]{1,0:T(8,128)(2,1)S(1)} fusion(bf16[7,128,3584]{2,1,0:T(8,128)(2,1)} %bitcast.70, bf16[1024,128,1]{1,0,2:T(8,128)(2,1)S(1)} %bitcast.65, f32[1024,128,7]{1,0,2:T(8,128)} %copy-done.1, f32[7,128]{1,0:T(8,128)S(1)} %broadcast_maximum_fusion, pred[128,1024]{0,1:T(8,128)(4,1)S(1)} %fusion.16, f32[7,128]{1,0:T(8,128)S(1)} %fusion.2), kind=kOutput, calls=%fused_computation.2 | convolution fusion | flops 1062240256 | bytes 11410432 | tf_op jit(solution)/shard_map/gqd,gde->qe/dot_general | solution.py:83
  43.3 1.3 %copy.20 = bf16[128,3584]{0,1:T(8,128)(2,1)} copy(bf16[128,3584]{1,0:T(8,128)(2,1)S(1)} %fusion) | data formatting | bytes 1835008
  44.6 0.0 reduce-scatter.4.cloned.1.call-update
  44.6 25.3 %reduce-scatter.4.cloned.1.call-done = bf16[896,128]{1,0:T(8,128)(2,1)} async-done(((bf16[3584,128]{1,0:T(8,128)(2,1)}), bf16[896,128]{1,0:T(8,128)(2,1)}) %reduce-scatter.4.cloned.1.call-update) | async-done | bytes 229392
  70.0 1.8 %copy.21 = bf16[128,896]{1,0:T(8,128)(2,1)} copy(bf16[128,896]{0,1:T(8,128)(2,1)} %bitcast.66) | data formatting | bytes 458752
  (14 shorter events, 0.2 us)
Async XLA Ops:
  6.5 19.0 %copy-start = (s32[1,8]{1,0:T(1,128)S(1)}, s32[1,8]{1,0:T(1,128)}, u32[]{:S(2)}) copy-start(s32[1,8]{1,0:T(1,128)} %param.14) | copy-start | bytes 100
  6.5 21.9 %copy-start.2 = (s32[1024]{0:T(1024)S(1)}, s32[1024]{0:T(1024)}, u32[]{:S(2)}) copy-start(s32[1024]{0:T(1024)} %param.13) | copy-start | bytes 12292
  6.5 63.4 %reduce-scatter.4.cloned.1.call-start = ((), (), s32[]{:S(2)}) async-start(), calls=%async_computation.1 | async-start | bytes 1146880
  10.1 5.3 %collective-permute-start = (bf16[1,2,128,128]{3,2,1,0:T(8,128)(2,1)S(1)}, bf16[1,2,128,128]{3,2,1,0:T(8,128)(2,1)S(1)}, u32[]{:S(2)}, u32[]{:S(2)}) collective-permute-start(bf16[1,2,128,128]{3,2,1,0:T(8,128)(2,1)S(1)} %maximum_bitcast_fusion.1), channel_id=1, source_target_pairs={{0,4},{4,0},{8,12},{12,8},{16,20},{20,16},{24,28},{28,24},{1,5},{5... | collective-permute-start | bytes 196616 | tf_op jit(solution)/shard_map/ppermute | solution.py:22
  15.4 5.1 %collective-permute-start.1 = (bf16[2,2,128,128]{3,2,1,0:T(8,128)(2,1)S(1)}, bf16[2,2,128,128]{3,2,1,0:T(8,128)(2,1)S(1)}, u32[]{:S(2)}, u32[]{:S(2)}) collective-permute-start(bf16[2,2,128,128]{3,2,1,0:T(8,128)(2,1)S(1)} %pad_maximum_fusion.1), channel_id=1, source_target_pairs={{0,8},{4,12},{8,0},{12,4},{16,24},{20,28},{24,16},{28,20},{1,9},{5... | collective-permute-start | bytes 393224 | tf_op jit(solution)/shard_map/ppermute | solution.py:22
  20.6 12.7 %collective-permute-start.2 = (bf16[4,2,128,128]{3,2,1,0:T(8,128)(2,1)S(1)}, bf16[4,2,128,128]{3,2,1,0:T(8,128)(2,1)S(1)}, u32[]{:S(2)}, u32[]{:S(2)}) collective-permute-start(bf16[4,2,128,128]{3,2,1,0:T(8,128)(2,1)S(1)} %pad_maximum_fusion), channel_id=1, source_target_pairs={{0,16},{4,20},{8,24},{12,28},{16,0},{20,4},{24,8},{28,12},{1,17},{... | collective-permute-start | bytes 786440 | tf_op jit(solution)/shard_map/ppermute | solution.py:22
  34.1 1.8 %copy-start.1 = (f32[1024,128,7]{1,0,2:T(8,128)}, f32[1024,128,7]{1,0,2:T(8,128)S(1)}, u32[]{:S(2)}) copy-start(f32[1024,128,7]{1,0,2:T(8,128)S(1)} %get-tuple-element.16) | copy-start | bytes 11010052
Sparse Core Ops, SparseCore 0:
  44.8 25.1 reduce-scatter.3
